TPU v7x, 128 devices: a whole 4x4x4 slice. The times are simulated.
128 devices in a mesh: row: 8 (over z, y_lo), col: 16 (over y_hi, x, core).
Axes of the slice: x: 4, y: 4 (y_hi: 2, y_lo: 2; y = y_hi * 2 + y_lo), z: 4, core: 2. Of those that a mesh axis runs over, the one named last changes fastest.
Arguments:
- spectra: bfloat16 [2048, 256, 512], P(('row', 'col')), may hold values from 0.05 to 20000
- sensor_ids: int32 [2048, 1], P(('row', 'col')), may hold values from 0 to 255, as said below
- permutation: int32 [2048], P(('row', 'col')), may hold values from 0 to 2047, as said below
- w_enc1: bfloat16 [2048, 256], replicated, may hold values from -0.125 to 0.125
- w_enc2: bfloat16 [1024, 256], replicated, may hold values from -0.1875 to 0.1875
- w_dec1: bfloat16 [256, 1024], replicated, may hold values from -0.25 to 0.25
- w_dec2: bfloat16 [256, 2048], replicated, may hold values from -0.25 to 0.25
Outputs:
- grad_enc1: float32 [2048, 256], replicated
- grad_enc2: float32 [1024, 256], replicated
- grad_dec1: float32 [256, 1024], replicated
- grad_dec2: float32 [256, 2048], replicated
Inputs may be any that keep to these rules, and one draw needn't show every extreme that they name: `sensor_ids`: every sensor from 0 to 255 recorded exactly 8 windows. A permutation of all slots; the 16 windows of the ingest device with indices (a, b) go to 16 different trainers, one to each trainer whose col index c has c // 2 = a; each trainer thus receives one window from each ingest device of one row index.
All inputs are finite; a program needn't handle non-finite values.
Results may differ from a plain program's by a relative error of at most 0.004.
Values may be sent and summed in bfloat16 or wider, within the bound.
No kernel may reach another device: no remote copies, remote signals or barrier semaphores. Data moves between devices by JAX's collectives and lax.ppermute only.
A program may use at most 192 MiB of HBM per device.

v0:
```python
import jax
import jax.numpy as jnp
from jax import lax
from jax.sharding import PartitionSpec as P

WIN_SENSOR = 8
EPS = 1e-05


def frame_taps(values):
    windows, length, channels = values.shape
    padded = jnp.pad(values, ((0, 0), (1, 1), (0, 0)))
    paired = padded.reshape(windows, length // 2 + 1, 2 * channels)
    return jnp.concatenate([paired[:, :-1], paired[:, 1:]], axis=2)


def fold_taps(stacked):
    windows, length, columns = stacked.shape
    channels = columns // 4
    pieces = stacked.reshape(windows, length, 4, channels)
    blank = jnp.zeros((windows, 1, channels), stacked.dtype)
    even_rows = pieces[:, :, 1] + jnp.concatenate([blank, pieces[:, :-1, 3]], axis=1)
    odd_rows = pieces[:, :, 2] + jnp.concatenate([pieces[:, 1:, 0], blank], axis=1)
    return jnp.stack([even_rows, odd_rows], axis=2).reshape(windows, 2 * length, channels)


def silu_slope(values):
    logistic = jax.nn.sigmoid(values)
    return logistic * (1.0 + values * (1.0 - logistic))


def forward_dot(values, weight):
    flat = values.reshape(-1, values.shape[-1])
    result = jnp.dot(flat, weight, preferred_element_type=jnp.float32)
    return result.reshape(values.shape[:-1] + (weight.shape[1],))


def backward_dot(values, weight):
    flat = values.reshape(-1, values.shape[-1])
    result = lax.dot_general(
        flat, weight, (((1,), (1,)), ((), ())), preferred_element_type=jnp.float32
    )
    return result.reshape(values.shape[:-1] + (weight.shape[0],))


def sensor_table(sensor_col, sensor_total):
    return (sensor_col[:, None] == jnp.arange(sensor_total, dtype=jnp.int32)[None, :]).astype(
        jnp.float32
    )


def standardize(log_power, table, center, factor):
    shift = jnp.dot(table, center, precision=lax.Precision.HIGHEST)
    stretch = jnp.dot(table, factor, precision=lax.Precision.HIGHEST)
    return ((log_power - shift[:, None, :]) * stretch[:, None, :]).astype(jnp.bfloat16)


def layer_sum(left, right):
    left_flat = left.reshape(-1, left.shape[-1])
    right_flat = right.reshape(-1, right.shape[-1])
    gradient = jnp.einsum("rk,ro->ko", left_flat, right_flat, preferred_element_type=jnp.float32)
    return gradient


def local(spectra, sensor_ids, permutation, w_enc1, w_enc2, w_dec1, w_dec2):
    window_count = spectra.shape[0]
    frame_count = spectra.shape[1]
    row_count = lax.axis_size("row")
    col_count = lax.axis_size("col")
    total_windows = window_count * row_count * col_count
    sensor_total = total_windows // WIN_SENSOR
    sensor_col = sensor_ids[:, 0]
    table = sensor_table(sensor_col, sensor_total)
    log_power = jnp.log1p(spectra.astype(jnp.float32))
    win_sums = jnp.sum(log_power, axis=1)
    win_squares = jnp.sum(log_power * log_power, axis=1)
    totals = jnp.einsum("ws,wb->sb", table, win_sums, precision=lax.Precision.HIGHEST)
    squares = jnp.einsum("ws,wb->sb", table, win_squares, precision=lax.Precision.HIGHEST)
    counts = jnp.sum(table, axis=0) * frame_count
    totals, squares, counts = lax.psum((totals, squares, counts), ("row", "col"))
    center = totals / counts[:, None]
    factor = lax.rsqrt(squares / counts[:, None] - center * center + EPS)
    payload = standardize(log_power, table, center, factor)
    labels = jnp.stack([permutation, sensor_col], axis=1)
    positions = jnp.arange(window_count, dtype=jnp.int32)
    ranking = jnp.argsort(labels[:, 0] // col_count // col_count * col_count + positions)
    payload, labels = (
        lax.all_to_all(payload[ranking], "row", split_axis=0, concat_axis=0, tiled=True),
        lax.all_to_all(labels[ranking], "row", split_axis=0, concat_axis=0, tiled=True),
    )
    ranking = jnp.argsort(labels[:, 0] // col_count % col_count)
    payload, labels = (
        lax.all_to_all(payload[ranking], "col", split_axis=0, concat_axis=0, tiled=True),
        lax.all_to_all(labels[ranking], "col", split_axis=0, concat_axis=0, tiled=True),
    )
    stem_taps = frame_taps(payload)
    enc1_pre = forward_dot(stem_taps, w_enc1)
    middle = jnp.mean(enc1_pre, axis=(0, 1))
    variance = jnp.mean(jnp.square(enc1_pre - middle), axis=(0, 1))
    inverse = lax.rsqrt(variance + EPS)
    enc1_hat = (enc1_pre - middle) * inverse
    enc1_out = jax.nn.silu(enc1_hat).astype(jnp.bfloat16)
    mid_taps = frame_taps(enc1_out)
    enc2_pre = forward_dot(mid_taps, w_enc2)
    enc2_out = jax.nn.silu(enc2_pre).astype(jnp.bfloat16)
    dec1_pre = fold_taps(forward_dot(enc2_out, w_dec1))
    dec1_out = jax.nn.silu(dec1_pre).astype(jnp.bfloat16)
    rebuilt = fold_taps(forward_dot(dec1_out, w_dec2))
    delta_out = ((rebuilt - payload.astype(jnp.float32)) / total_windows).astype(jnp.bfloat16)
    out_taps = frame_taps(delta_out)
    grad_dec2 = layer_sum(dec1_out, out_taps)
    delta_dec1 = (backward_dot(out_taps, w_dec2) * silu_slope(dec1_pre)).astype(jnp.bfloat16)
    dec_taps = frame_taps(delta_dec1)
    grad_dec1 = layer_sum(enc2_out, dec_taps)
    delta_enc2 = (backward_dot(dec_taps, w_dec1) * silu_slope(enc2_pre)).astype(jnp.bfloat16)
    grad_enc2 = layer_sum(mid_taps, delta_enc2)
    back_enc1 = fold_taps(backward_dot(delta_enc2, w_enc2)) * silu_slope(enc1_hat)
    first_mean = jnp.mean(back_enc1, axis=(0, 1))
    second_mean = jnp.mean(back_enc1 * enc1_hat, axis=(0, 1))
    delta_enc1 = ((back_enc1 - first_mean - enc1_hat * second_mean) * inverse).astype(jnp.bfloat16)
    grad_enc1 = layer_sum(stem_taps, delta_enc1)
    grad_enc1, grad_enc2, grad_dec1, grad_dec2 = lax.psum(
        (grad_enc1, grad_enc2, grad_dec1, grad_dec2), ("row", "col")
    )
    return (grad_enc1, grad_enc2, grad_dec1, grad_dec2)


def solution(mesh):
    return jax.shard_map(
        local,
        mesh=mesh,
        in_specs=(
            P(("row", "col"), None, None),
            P(("row", "col"), None),
            P(("row", "col")),
            P(),
            P(),
            P(),
            P(),
        ),
        out_specs=(P(), P(), P(), P()),
        check_vma=False,
    )
```

profile of v0, /device:TPU:1, one launch (start us, length us, event | category | flops | bytes accessed | tf_op | source)
XLA Modules:
  0.0 608.6 jit_solution(8705638095930346824)
XLA Ops:
  7.2 5.9 fusion.2
  18.4 6.9 %all-to-all-start.1 = ((s32[8,2,2]{1,2,0:T(2,128)}), s32[8,2,2]{1,2,0:T(2,128)S(1)}, u32[]{:S(2)}, u32[]{:S(2)}) async-start(s32[8,2,2]{1,2,0:T(2,128)} %copy.99), calls=%async_computation.1 | async-start | bytes 16384 | tf_op jit(solution)/shard_map/all_to_all | solution.py:89
  25.4 67.2 %psum.50 = f32[256]{0:T(256)S(1)} all-reduce(f32[256]{0:T(256)S(1)} %broadcast_multiply_fusion.3), channel_id=1, replica_groups=mesh['row'=8,'col'=16] {'row','col'}, use_global_device_ids=true, to_apply=%region_3.0 | all-reduce | flops 256 | bytes 2048 | tf_op jit(solution)/shard_map/psum | solution.py:80
  92.6 74.5 %all-reduce.17.cloned.1.call-done = (f32[256,512]{1,0:T(8,128)}, f32[256,512]{1,0:T(8,128)}) async-done(((f32[256,512]{1,0:T(8,128)}, f32[256,512]{1,0:T(8,128)}), (f32[256,512]{1,0:T(8,128)}, f32[256,512]{1,0:T(8,128)})) %all-reduce.17.cloned.1.call-update) | async-done | bytes 1048592 | tf_op jit(solution)/shard_map/psum | solution.py:80
  170.4 5.4 multiply_convert_fusion
  175.8 4.9 gather_fusion
  180.7 4.6 all-to-all-start
  186.7 48.3 %all-to-all-done = bf16[16,256,512]{2,1,0:T(8,128)(2,1)} async-done(((bf16[16,256,512]{2,1,0:T(8,128)(2,1)}), bf16[16,256,512]{2,1,0:T(8,128)(2,1)}, u32[]{:S(2)}, u32[]{:S(2)}) %all-to-all-start) | async-done | bytes 4194336 | tf_op jit(solution)/shard_map/all_to_all | solution.py:88
  234.9 5.0 gather_fusion.2
  239.9 6.1 %all-to-all-start.2 = ((bf16[16,256,512]{2,1,0:T(8,128)(2,1)}), bf16[16,256,512]{2,1,0:T(8,128)(2,1)}, u32[]{:S(2)}, u32[]{:S(2)}) async-start(bf16[16,256,512]{2,1,0:T(8,128)(2,1)} %gather_fusion.2), calls=%async_computation.2 | async-start | bytes 8388608 | tf_op jit(solution)/shard_map/all_to_all | solution.py:93
  248.6 53.3 %all-to-all-done.2 = bf16[16,256,512]{2,1,0:T(8,128)(2,1)} async-done(((bf16[16,256,512]{2,1,0:T(8,128)(2,1)}), bf16[16,256,512]{2,1,0:T(8,128)(2,1)}, u32[]{:S(2)}, u32[]{:S(2)}) %all-to-all-start.2) | async-done | bytes 4194336 | tf_op jit(solution)/shard_map/all_to_all | solution.py:93
  301.9 5.9 pad.20
  307.9 7.2 %reshape.92 = bf16[16,129,1024]{2,1,0:T(8,128)(2,1)} reshape(bf16[16,258,512]{2,1,0:T(8,128)(2,1)} %pad.20) | data formatting | bytes 8454144 | tf_op jit(solution)/shard_map/reshape | solution.py:13
  315.1 4.4 fusion.66
  344.7 4.8 slice_bitcast_fusion.2
  352.9 11.7 %fusion.10 = (f32[16,128,1,512]{3,1,0,2:T(8,128)}, f32[16,128,1,512]{3,1,0,2:T(8,128)}) fusion(f32[16,128,4,512]{3,1,2,0:T(8,128)} %copy-done.2, f32[16,127,512]{2,1,0:T(8,128)} %get-tuple-element.20, f32[16,127,512]{2,1,0:T(8,128)} %get-tuple-element.21), kind=kLoop, calls=%fused_computation.24 | loop fusion | flops 2097152 | bytes 25100288 | tf_op jit(solution)/shard_map/stack | solution.py:24
  364.6 4.5 pad_maximum_fusion.1
  369.1 4.9 copy.111
  374.0 10.0 %fusion.1 = bf16[16,256,512]{2,1,0:T(8,128)(2,1)} fusion(f32[16,256,512]{2,0,1:T(8,128)S(1)} %bitcast.146, bf16[16,256,512]{2,1,0:T(8,128)(2,1)} %all-to-all-done.2), kind=kLoop, calls=%fused_computation.8 | loop fusion | flops 8388608 | bytes 16777216 | tf_op jit(solution)/shard_map/convert_element_type | solution.py:109
  384.0 5.9 pad.22
  389.9 7.2 %reshape.95 = bf16[16,129,1024]{2,1,0:T(8,128)(2,1)} reshape(bf16[16,258,512]{2,1,0:T(8,128)(2,1)} %pad.22) | data formatting | bytes 8454144 | tf_op jit(solution)/shard_map/reshape | solution.py:13
  397.1 4.7 fusion.65
  429.5 7.7 %fusion.11 = f32[2048,256]{1,0:T(8,128)} fusion(bf16[16,128,1024]{2,1,0:T(8,128)(2,1)} %copy-done.6, bf16[16,128,1024]{2,1,0:T(8,128)(2,1)} %copy-done.5, f32[16,128,256]{2,1,0:T(8,128)S(1)} %get-tuple-element.41, f32[256]{0:T(256)S(1)} %get-tuple-element.42, f32[256]{0:T(256)S(1)} %get-tuple-element.43, f32[256]{0:T(256)S(1)} %add_rsqrt_fusion, ...), kind=kOutput, calls=%fused_computation.25 | convolution fusion | flops 2172125184 | bytes 14684160 | tf_op jit(solution)/shard_map/rk,ro->ko/dot_general | solution.py:61
  437.2 157.9 %all-reduce.15.cloned.1.call-done = (f32[2048,256]{1,0:T(8,128)}, f32[1024,256]{1,0:T(8,128)}, f32[256,1024]{1,0:T(8,128)}, f32[256,2048]{1,0:T(8,128)}) async-done(((f32[2048,256]{1,0:T(8,128)}, f32[1024,256]{1,0:T(8,128)}, f32[256,1024]{1,0:T(8,128)}, f32[256,2048]{1,0:T(8,128)}), (f32[2048,256]{1,0:T(8,128)}, f32[1024,256]{1,0:T(8,128)}, f32[256,1024]{1,0:T(8,128)}, ...) | async-done | bytes 6291472 | tf_op jit(solution)/shard_map/psum | solution.py:122
  (116 shorter events, 75.2 us)
Async XLA Ops:
  7.2 312.4 %copy-start = (bf16[2048,256]{1,0:T(8,128)(2,1)S(1)}, bf16[2048,256]{1,0:T(8,128)(2,1)}, u32[]{:S(2)}) copy-start(bf16[2048,256]{1,0:T(8,128)(2,1)} %param.10) | copy-start | bytes 3145732
  7.2 5.9 copy-start.21
  7.2 8.5 %copy-start.22 = (s32[16]{0:T(128)S(1)}, s32[16]{0:T(128)}, u32[]{:S(2)}) copy-start(s32[16]{0:T(128)} %param.9) | copy-start | bytes 196
  7.2 159.9 %all-reduce.17.cloned.1.call-start = ((), (), s32[]{:S(2)}) async-start(), calls=%async_computation.4 | async-start | bytes 2097152 | tf_op jit(solution)/shard_map/psum | solution.py:80
  18.4 162.3 %all-to-all-start.1 = ((s32[8,2,2]{1,2,0:T(2,128)}), s32[8,2,2]{1,2,0:T(2,128)S(1)}, u32[]{:S(2)}, u32[]{:S(2)}) async-start(s32[8,2,2]{1,2,0:T(2,128)} %copy.99), calls=%async_computation.1 | async-start | bytes 16384 | tf_op jit(solution)/shard_map/all_to_all | solution.py:89
  167.1 3.2 copy-start.3
  180.7 54.2 %all-to-all-start = ((bf16[16,256,512]{2,1,0:T(8,128)(2,1)}), bf16[16,256,512]{2,1,0:T(8,128)(2,1)}, u32[]{:S(2)}, u32[]{:S(2)}) async-start(bf16[16,256,512]{2,1,0:T(8,128)(2,1)} %gather_fusion), calls=%async_computation | async-start | bytes 8388608 | tf_op jit(solution)/shard_map/all_to_all | solution.py:88
  239.9 6.4 %copy-start.18 = (bf16[256,1024]{1,0:T(8,128)(2,1)S(1)}, bf16[256,1024]{1,0:T(8,128)(2,1)}, u32[]{:S(2)}) copy-start(bf16[256,1024]{1,0:T(8,128)(2,1)} %param.12) | copy-start | bytes 1572868
  239.9 7.4 %copy-start.9 = (bf16[256,2048]{1,0:T(8,128)(2,1)S(1)}, bf16[256,2048]{1,0:T(8,128)(2,1)}, u32[]{:S(2)}) copy-start(bf16[256,2048]{1,0:T(8,128)(2,1)} %param.13) | copy-start | bytes 3145732
  239.9 62.0 %all-to-all-start.2 = ((bf16[16,256,512]{2,1,0:T(8,128)(2,1)}), bf16[16,256,512]{2,1,0:T(8,128)(2,1)}, u32[]{:S(2)}, u32[]{:S(2)}) async-start(bf16[16,256,512]{2,1,0:T(8,128)(2,1)} %gather_fusion.2), calls=%async_computation.2 | async-start | bytes 8388608 | tf_op jit(solution)/shard_map/all_to_all | solution.py:93
  246.0 349.1 %all-reduce.15.cloned.1.call-start = ((), (), s32[]{:S(2)}) async-start(), calls=%async_computation.3 | async-start | bytes 12582912 | tf_op jit(solution)/shard_map/psum | solution.py:122
  319.5 3.2 copy-start.6
  327.4 4.3 copy-start.20
  329.5 3.0 copy-start.13
  329.5 3.0 copy-start.15
  344.7 8.2 %copy-start.2 = (f32[16,128,4,512]{3,1,2,0:T(8,128)}, f32[16,128,4,512]{3,1,2,0:T(8,128)S(1)}, u32[]{:S(2)}) copy-start(f32[16,128,4,512]{3,1,2,0:T(8,128)S(1)} %fusion.24) | copy-start | bytes 50331652
  397.1 4.7 copy-start.7
  397.1 4.7 copy-start.10
  409.7 4.6 copy-start.19
  426.8 2.7 copy-start.4
  595.1 3.2 copy-start.12
  595.1 4.2 copy-start.11
  595.1 5.2 copy-start.8
  595.1 6.5 %copy-start.1 = (bf16[2048,256]{1,0:T(8,128)(2,1)S(1)}, bf16[2048,256]{1,0:T(8,128)(2,1)}, u32[]{:S(2)}) copy-start(bf16[2048,256]{1,0:T(8,128)(2,1)} %param.10) | copy-start | bytes 3145732
  (6 other events, 11.0 us)
Sparse Core Ops, SparseCore 0:
  15.9 151.2 all-reduce.16
  437.3 157.7 all-reduce.14
where the time goes:
time: 618 us; the launch traced here: 609 us
  waiting for transfers between devices  334 us (54%)
  local copies, waits for them, and re-layouts  95.4 us (15%)
  blocking collectives  67.2 us (11%)
  other arithmetic  45.3 us (7%)
  matrix products  34.1 us (6%)
  starting transfers between devices  17.8 us (3%)
  between operations  14.7 us (2%)
    psum x1, waiting for transfers between devices, local(): lax.psum((grad_enc1, grad_enc2, grad_dec1, grad_dec2), ('row', 'col'))  158 us
    psum x1, waiting for transfers between devices, local(): lax.psum((totals, squares, counts), ('row', 'col'))  74.5 us
    psum x1, blocking collectives, local(): lax.psum((totals, squares, counts), ('row', 'col'))  67.2 us
    all_to_all x1, waiting for transfers between devices, local(): lax.all_to_all(payload[ranking], 'col', split_axis=0, concat_axis=0, tile...  53.3 us
    all_to_all x1, waiting for transfers between devices, local(): lax.all_to_all(payload[ranking], 'row', split_axis=0, concat_axis=0, tile...  48.3 us
    reshape x4, local copies, waits for them, and re-layouts, frame_taps(): paired = padded.reshape(windows, length // 2 + 1, 2 * channels)  19.1 us
    another operation x5, other arithmetic, fold_taps(): jnp.stack([even_rows, odd_rows], axis=2)  17 us
    dot_general x4, matrix products, layer_sum(): jnp.einsum('rk,ro->ko', left_flat, right_flat, preferred_element_type=jnp...  14.9 us
  transfers between devices with their start and end apart: 5, of which 4 were waited for; matrix products, arithmetic and copies ran while one was open for 3% of the time, Pallas kernels for 0%

commit v1 on v0

--- a/solution.py
+++ b/solution.py
@@ -1,3 +1,4 @@
+import functools
 import jax
 import jax.numpy as jnp
 from jax import lax
@@ -5,6 +6,13 @@
 
 WIN_SENSOR = 8
 EPS = 1e-05
+
+
+def _arrange_state(t0, lane_axis, bus_axis):
+    return lax.psum(lax.psum(t0, axis_name=bus_axis), axis_name=lane_axis)
+
+
+meet_roots = functools.partial(_arrange_state, lane_axis="row", bus_axis="col")
 
 
 def frame_taps(values):
@@ -77,7 +85,7 @@
     totals = jnp.einsum("ws,wb->sb", table, win_sums, precision=lax.Precision.HIGHEST)
     squares = jnp.einsum("ws,wb->sb", table, win_squares, precision=lax.Precision.HIGHEST)
     counts = jnp.sum(table, axis=0) * frame_count
-    totals, squares, counts = lax.psum((totals, squares, counts), ("row", "col"))
+    totals, squares, counts = meet_roots((totals, squares, counts))
     center = totals / counts[:, None]
     factor = lax.rsqrt(squares / counts[:, None] - center * center + EPS)
     payload = standardize(log_power, table, center, factor)

time: 618 us -> 691 us (1.12)
  waiting for transfers between devices: 334 us -> 419 us
  blocking collectives: 67.2 us -> 51.6 us
    psum x1 -> x2, waiting for transfers between devices: 74.5 us -> 166 us  [_arrange_state(): return lax.psum(lax.psum(t0, axis_name=bus_axis), axis_name=lane_axis)]
    psum x1 -> x2, blocking collectives: 67.2 us -> 51.6 us  [_arrange_state(): return lax.psum(lax.psum(t0, axis_name=bus_axis), axis_name=lane_axis)]
    all_to_all x1, starting transfers between devices: 6.14 us -> 13.5 us  [local(): lax.all_to_all(payload[ranking], 'col', split_axis=0, concat_axis=0, tile...]
  transfers between devices with their start and end apart: 5 -> 6, of which waited for: 4 -> 5; matrix products, arithmetic and copies ran while one was open for 3% -> 3% of each run, Pallas kernels for 0% -> 0%
where the time goes in v1:
time: 691 us; the launch traced here: 683 us
  waiting for transfers between devices  419 us (61%)
  local copies, waits for them, and re-layouts  96.2 us (14%)
  blocking collectives  51.6 us (7%)
  other arithmetic  45.3 us (7%)
  matrix products  34.1 us (5%)
  starting transfers between devices  22.5 us (3%)
  between operations  14.4 us (2%)
    psum x2, waiting for transfers between devices, _arrange_state(): return lax.psum(lax.psum(t0, axis_name=bus_axis), axis_name=lane_axis)  166 us
    psum x1, waiting for transfers between devices, local(): lax.psum((grad_enc1, grad_enc2, grad_dec1, grad_dec2), ('row', 'col'))  157 us
    all_to_all x1, waiting for transfers between devices, local(): lax.all_to_all(payload[ranking], 'col', split_axis=0, concat_axis=0, tile...  53.3 us
    psum x2, blocking collectives, _arrange_state(): return lax.psum(lax.psum(t0, axis_name=bus_axis), axis_name=lane_axis)  51.6 us
    all_to_all x1, waiting for transfers between devices, local(): lax.all_to_all(payload[ranking], 'row', split_axis=0, concat_axis=0, tile...  42.1 us
    reshape x4, local copies, waits for them, and re-layouts, frame_taps(): paired = padded.reshape(windows, length // 2 + 1, 2 * channels)  19.1 us
    another operation x5, other arithmetic, fold_taps(): jnp.stack([even_rows, odd_rows], axis=2)  17 us
    dot_general x4, matrix products, layer_sum(): jnp.einsum('rk,ro->ko', left_flat, right_flat, preferred_element_type=jnp...  14.9 us
  transfers between devices with their start and end apart: 6, of which 5 were waited for; matrix products, arithmetic and copies ran while one was open for 3% of the time, Pallas kernels for 0%

profile of v1, /device:TPU:1, one launch (start us, length us, event | category | flops | bytes accessed | tf_op | source)
XLA Modules:
  0.0 682.7 jit_solution(3585785852350820958)
XLA Ops:
  7.2 5.9 fusion.2
  15.8 143.7 %all-reduce.19.cloned.1.call-done = (f32[256,512]{1,0:T(8,128)}, f32[256,512]{1,0:T(8,128)}) async-done(((f32[256,512]{1,0:T(8,128)}, f32[256,512]{1,0:T(8,128)}), (f32[256,512]{1,0:T(8,128)}, f32[256,512]{1,0:T(8,128)})) %all-reduce.19.cloned.1.call-update) | async-done | bytes 1048592 | tf_op jit(solution)/shard_map/psum | solution.py:12
  166.5 34.2 %psum.72 = f32[256]{0:T(256)S(1)} all-reduce(f32[256]{0:T(256)S(1)} %broadcast_multiply_fusion.3), channel_id=1, replica_groups=mesh['row'=8,'col'=16] {'col'}, use_global_device_ids=true, to_apply=%region_4.0 | all-reduce | flops 256 | bytes 2048 | tf_op jit(solution)/shard_map/psum | solution.py:12
  200.7 17.3 %psum.73 = f32[256]{0:T(256)S(1)} all-reduce(f32[256]{0:T(256)S(1)} %psum.72), channel_id=1, replica_groups=mesh['row'=8,'col'=16] {'row'}, use_global_device_ids=true, to_apply=%region_5.0 | all-reduce | flops 256 | bytes 2048 | tf_op jit(solution)/shard_map/psum | solution.py:12
  218.0 22.2 %all-reduce.21.cloned.1.call-done = (f32[256,512]{1,0:T(8,128)}, f32[256,512]{1,0:T(8,128)}) async-done(((f32[256,512]{1,0:T(8,128)}, f32[256,512]{1,0:T(8,128)}), (f32[256,512]{1,0:T(8,128)}, f32[256,512]{1,0:T(8,128)})) %all-reduce.21.cloned.1.call-update) | async-done | bytes 1048592 | tf_op jit(solution)/shard_map/psum | solution.py:12
  243.4 5.4 multiply_convert_fusion
  248.8 4.9 gather_fusion
  253.8 4.6 all-to-all-start
  259.7 42.1 %all-to-all-done = bf16[16,256,512]{2,1,0:T(8,128)(2,1)} async-done(((bf16[16,256,512]{2,1,0:T(8,128)(2,1)}), bf16[16,256,512]{2,1,0:T(8,128)(2,1)}, u32[]{:S(2)}, u32[]{:S(2)}) %all-to-all-start) | async-done | bytes 4194336 | tf_op jit(solution)/shard_map/all_to_all | solution.py:96
  301.8 4.9 gather_fusion.2
  306.7 13.5 %all-to-all-start.2 = ((bf16[16,256,512]{2,1,0:T(8,128)(2,1)}), bf16[16,256,512]{2,1,0:T(8,128)(2,1)}, u32[]{:S(2)}, u32[]{:S(2)}) async-start(bf16[16,256,512]{2,1,0:T(8,128)(2,1)} %gather_fusion.2), calls=%async_computation.2 | async-start | bytes 8388608 | tf_op jit(solution)/shard_map/all_to_all | solution.py:101
  322.8 53.3 %all-to-all-done.2 = bf16[16,256,512]{2,1,0:T(8,128)(2,1)} async-done(((bf16[16,256,512]{2,1,0:T(8,128)(2,1)}), bf16[16,256,512]{2,1,0:T(8,128)(2,1)}, u32[]{:S(2)}, u32[]{:S(2)}) %all-to-all-start.2) | async-done | bytes 4194336 | tf_op jit(solution)/shard_map/all_to_all | solution.py:101
  376.2 5.9 pad.20
  382.1 7.2 %reshape.92 = bf16[16,129,1024]{2,1,0:T(8,128)(2,1)} reshape(bf16[16,258,512]{2,1,0:T(8,128)(2,1)} %pad.20) | data formatting | bytes 8454144 | tf_op jit(solution)/shard_map/reshape | solution.py:21
  418.9 4.8 slice_bitcast_fusion.2
  427.9 11.7 %fusion.10 = (f32[16,128,1,512]{3,1,0,2:T(8,128)}, f32[16,128,1,512]{3,1,0,2:T(8,128)}) fusion(f32[16,128,4,512]{3,1,2,0:T(8,128)} %copy-done.2, f32[16,127,512]{2,1,0:T(8,128)} %get-tuple-element.22, f32[16,127,512]{2,1,0:T(8,128)} %get-tuple-element.23), kind=kLoop, calls=%fused_computation.24 | loop fusion | flops 2097152 | bytes 25100288 | tf_op jit(solution)/shard_map/stack | solution.py:32
  439.6 4.5 pad_maximum_fusion.1
  444.0 4.9 copy.111
  448.9 10.0 %fusion.1 = bf16[16,256,512]{2,1,0:T(8,128)(2,1)} fusion(f32[16,256,512]{2,0,1:T(8,128)S(1)} %bitcast.146, bf16[16,256,512]{2,1,0:T(8,128)(2,1)} %all-to-all-done.2), kind=kLoop, calls=%fused_computation.8 | loop fusion | flops 8388608 | bytes 16777216 | tf_op jit(solution)/shard_map/convert_element_type | solution.py:117
  458.9 5.9 pad.22
  464.8 7.2 %reshape.95 = bf16[16,129,1024]{2,1,0:T(8,128)(2,1)} reshape(bf16[16,258,512]{2,1,0:T(8,128)(2,1)} %pad.22) | data formatting | bytes 8454144 | tf_op jit(solution)/shard_map/reshape | solution.py:21
  472.0 4.7 fusion.65
  504.5 7.7 %fusion.11 = f32[2048,256]{1,0:T(8,128)} fusion(bf16[16,128,1024]{2,1,0:T(8,128)(2,1)} %copy-done.6, bf16[16,128,1024]{2,1,0:T(8,128)(2,1)} %copy-done.5, f32[16,128,256]{2,1,0:T(8,128)S(1)} %get-tuple-element.43, f32[256]{0:T(256)S(1)} %get-tuple-element.44, f32[256]{0:T(256)S(1)} %get-tuple-element.45, f32[256]{0:T(256)S(1)} %add_rsqrt_fusion, ...), kind=kOutput, calls=%fused_computation.25 | convolution fusion | flops 2172125184 | bytes 14684160 | tf_op jit(solution)/shard_map/rk,ro->ko/dot_general | solution.py:69
  512.2 157.4 %all-reduce.17.cloned.1.call-done = (f32[2048,256]{1,0:T(8,128)}, f32[1024,256]{1,0:T(8,128)}, f32[256,1024]{1,0:T(8,128)}, f32[256,2048]{1,0:T(8,128)}) async-done(((f32[2048,256]{1,0:T(8,128)}, f32[1024,256]{1,0:T(8,128)}, f32[256,1024]{1,0:T(8,128)}, f32[256,2048]{1,0:T(8,128)}), (f32[2048,256]{1,0:T(8,128)}, f32[1024,256]{1,0:T(8,128)}, f32[256,1024]{1,0:T(8,128)}, ...) | async-done | bytes 6291472 | tf_op jit(solution)/shard_map/psum | solution.py:130
  (120 shorter events, 84.5 us)
Async XLA Ops:
  7.2 386.6 %copy-start = (bf16[2048,256]{1,0:T(8,128)(2,1)S(1)}, bf16[2048,256]{1,0:T(8,128)(2,1)}, u32[]{:S(2)}) copy-start(bf16[2048,256]{1,0:T(8,128)(2,1)} %param.10) | copy-start | bytes 3145732
  7.2 6.0 copy-start.21
  7.2 152.3 %copy-start.22 = (s32[16]{0:T(128)S(1)}, s32[16]{0:T(128)}, u32[]{:S(2)}) copy-start(s32[16]{0:T(128)} %param.9) | copy-start | bytes 196
  7.2 152.3 %all-reduce.19.cloned.1.call-start = ((), (), s32[]{:S(2)}) async-start(), calls=%async_computation.4 | async-start | bytes 2097152 | tf_op jit(solution)/shard_map/psum | solution.py:12
  15.7 224.4 %all-reduce.21.cloned.1.call-start = ((), (), s32[]{:S(2)}) async-start(), calls=%async_computation.5 | async-start | bytes 2097152 | tf_op jit(solution)/shard_map/psum | solution.py:12
  162.2 91.6 %all-to-all-start.1 = ((s32[8,2,2]{1,2,0:T(2,128)}), s32[8,2,2]{1,2,0:T(2,128)S(1)}, u32[]{:S(2)}, u32[]{:S(2)}) async-start(s32[8,2,2]{1,2,0:T(2,128)} %copy.99), calls=%async_computation.1 | async-start | bytes 16384 | tf_op jit(solution)/shard_map/all_to_all | solution.py:97
  240.2 3.2 copy-start.3
  253.8 48.0 %all-to-all-start = ((bf16[16,256,512]{2,1,0:T(8,128)(2,1)}), bf16[16,256,512]{2,1,0:T(8,128)(2,1)}, u32[]{:S(2)}, u32[]{:S(2)}) async-start(bf16[16,256,512]{2,1,0:T(8,128)(2,1)} %gather_fusion), calls=%async_computation | async-start | bytes 8388608 | tf_op jit(solution)/shard_map/all_to_all | solution.py:96
  306.7 13.7 %copy-start.18 = (bf16[256,1024]{1,0:T(8,128)(2,1)S(1)}, bf16[256,1024]{1,0:T(8,128)(2,1)}, u32[]{:S(2)}) copy-start(bf16[256,1024]{1,0:T(8,128)(2,1)} %param.12) | copy-start | bytes 1572868
  306.7 14.8 %copy-start.9 = (bf16[256,2048]{1,0:T(8,128)(2,1)S(1)}, bf16[256,2048]{1,0:T(8,128)(2,1)}, u32[]{:S(2)}) copy-start(bf16[256,2048]{1,0:T(8,128)(2,1)} %param.13) | copy-start | bytes 3145732
  306.7 69.4 %all-to-all-start.2 = ((bf16[16,256,512]{2,1,0:T(8,128)(2,1)}), bf16[16,256,512]{2,1,0:T(8,128)(2,1)}, u32[]{:S(2)}, u32[]{:S(2)}) async-start(bf16[16,256,512]{2,1,0:T(8,128)(2,1)} %gather_fusion.2), calls=%async_computation.2 | async-start | bytes 8388608 | tf_op jit(solution)/shard_map/all_to_all | solution.py:101
  320.2 349.3 %all-reduce.17.cloned.1.call-start = ((), (), s32[]{:S(2)}) async-start(), calls=%async_computation.3 | async-start | bytes 12582912 | tf_op jit(solution)/shard_map/psum | solution.py:130
  393.7 3.2 copy-start.6
  401.6 4.3 copy-start.20
  403.7 3.0 copy-start.13
  403.8 3.0 copy-start.15
  418.9 9.0 %copy-start.2 = (f32[16,128,4,512]{3,1,2,0:T(8,128)}, f32[16,128,4,512]{3,1,2,0:T(8,128)S(1)}, u32[]{:S(2)}) copy-start(f32[16,128,4,512]{3,1,2,0:T(8,128)S(1)} %fusion.24) | copy-start | bytes 50331652
  472.0 4.7 copy-start.7
  472.0 4.7 copy-start.10
  484.7 4.6 copy-start.19
  669.5 3.2 copy-start.12
  669.5 4.2 copy-start.11
  669.5 5.2 copy-start.8
  669.5 6.5 copy-start.1
  (7 other events, 13.7 us)
Sparse Core Ops, SparseCore 0:
  15.9 143.5 all-reduce.18
  162.2 77.9 all-reduce.20
  512.3 157.1 all-reduce.16
